TPU v7x, 256 devices: a whole 4x4x8 slice. The times are simulated.
256 devices in a mesh: seq: 16 (over y, x), chan: 16 (over z, core).
Axes of the slice: x: 4, y: 4, z: 8, core: 2. Of those that a mesh axis runs over, the one named last changes fastest.
Arguments:
- tokens: bfloat16 [57344, 2048], P('seq', 'chan'), may hold values from -6 to 6
- w_query: bfloat16 [2048, 256], replicated, may hold values from -0.125 to 0.125
- w_key: bfloat16 [2048, 256], replicated, may hold values from -0.125 to 0.125
- w_value: bfloat16 [2048, 2048], P(None, 'chan'), may hold values from -0.125 to 0.125
- w_out: bfloat16 [2048, 2048], replicated, may hold values from -0.125 to 0.125
- gain: float32 [2048], replicated, may hold values from 0.1 to 1.9
Outputs:
- mixed: bfloat16 [57344, 2048], P('seq', 'chan')
All inputs are finite; a program needn't handle non-finite values.
Results may differ from a plain program's by a relative error of at most 0.019.
Values may be sent and summed in bfloat16 or wider, within the bound.
A program may use at most 128 MiB of HBM per device.

v0:
```python
import jax
import jax.numpy as jnp
from jax import lax
from jax.sharding import PartitionSpec as P

HEADS = 16
FEAT = 16
HEAD_DIM = 128
BLOCK = 896


def feature_parts(rows):
    linear = rows * FEAT ** (-0.25)
    square = (rows[..., :, None] * rows[..., None, :]).reshape(rows.shape[:-1] + (FEAT * FEAT,)) * (
        2.0 * FEAT
    ) ** (-0.5)
    return (linear, square)


def per_device(tokens, w_query, w_key, w_value, w_out, gain):
    highest = lax.Precision.HIGHEST
    groups = lax.axis_size("chan")
    per_group = HEADS // groups
    my_group = lax.axis_index("chan")
    my_slab = lax.axis_index("seq")
    tok_rows = tokens.shape[0]
    query_cols = per_group * FEAT
    value_cols = per_group * HEAD_DIM
    query_mine = lax.dynamic_slice_in_dim(w_query, my_group * query_cols, query_cols, 1)
    key_mine = lax.dynamic_slice_in_dim(w_key, my_group * query_cols, query_cols, 1)
    initial = (
        jnp.zeros((tok_rows, query_cols), jnp.float32),
        jnp.zeros((tok_rows, query_cols), jnp.float32),
        jnp.zeros((tok_rows, value_cols), jnp.float32),
    )
    piece = lax.all_gather(tokens, "chan", axis=1, tiled=True)
    query_sum, key_sum, value_sum = tuple(
        (
            jnp.dot(piece, weight, preferred_element_type=jnp.float32)
            for weight in (query_mine, key_mine, w_value)
        )
    )
    query_rows = query_sum.astype(jnp.bfloat16)
    key_rows = key_sum.astype(jnp.bfloat16)
    value_rows = value_sum.astype(jnp.bfloat16)
    blocks = tok_rows // BLOCK
    query_blocks = query_rows.reshape(blocks, BLOCK, per_group, FEAT)
    key_blocks = key_rows.reshape(blocks, BLOCK, per_group, FEAT)
    value_blocks = value_rows.reshape(blocks, BLOCK, per_group, HEAD_DIM)
    value_f32 = value_blocks.astype(jnp.float32)
    key_linear, key_square = feature_parts(key_blocks.astype(jnp.float32))
    own_zero = jnp.sum(value_f32, axis=1)
    own_one = jnp.einsum("bthf,bthe->bhfe", key_linear, value_f32, precision=highest)
    own_two = jnp.einsum("bthf,bthe->bhfe", key_square, value_f32, precision=highest)
    own = (own_zero, own_one, own_two)
    slab_total = tuple((jnp.sum(member, axis=0) for member in own))
    initial = tuple((jnp.zeros_like(member) for member in slab_total))
    pieces = (
        lax.all_gather(slab_total[0][None].astype(jnp.bfloat16), "seq", axis=0, tiled=True).astype(
            jnp.float32
        ),
        lax.all_gather(slab_total[1][None].astype(jnp.bfloat16), "seq", axis=0, tiled=True).astype(
            jnp.float32
        ),
        lax.all_gather(slab_total[2][None].astype(jnp.bfloat16), "seq", axis=0, tiled=True).astype(
            jnp.float32
        ),
    )
    count = pieces[0].shape[0]
    order = jnp.arange(count, dtype=jnp.int32)
    earlier_mask = order < my_slab
    prefix = tuple(
        (
            total
            + jnp.sum(
                jnp.where(earlier_mask.reshape((count,) + (1,) * (piece.ndim - 1)), piece, 0.0),
                axis=0,
            )
            for total, piece in zip(initial, pieces)
        )
    )
    earlier = tuple(
        (
            jnp.concatenate([jnp.zeros_like(member[:1]), jnp.cumsum(member, axis=0)[:-1]], axis=0)
            + base[None]
            for member, base in zip(own, prefix)
        )
    )
    query_linear, query_square = feature_parts(query_blocks.astype(jnp.float32))
    inter = earlier[0][:, None] + jnp.einsum(
        "bthf,bhfe->bthe", query_linear, earlier[1], precision=highest
    )
    inter = inter + jnp.einsum("bthf,bhfe->bthe", query_square, earlier[2], precision=highest)
    scores = jnp.einsum(
        "bthf,bshf->bhts", query_blocks, key_blocks, preferred_element_type=jnp.float32
    ) * FEAT ** (-0.5)
    kernel = 1.0 + scores + 0.5 * scores * scores
    causal = jnp.arange(BLOCK)[:, None] >= jnp.arange(BLOCK)[None, :]
    weights = jnp.where(causal, kernel, 0.0).astype(jnp.bfloat16)
    intra = jnp.einsum("bhts,bshe->bthe", weights, value_blocks, preferred_element_type=jnp.float32)
    numerator = (intra + inter).reshape(tok_rows, per_group, HEAD_DIM)
    gain_mine = lax.dynamic_slice_in_dim(gain, my_group * value_cols, value_cols, 0).reshape(
        per_group, HEAD_DIM
    )
    mean_square = jnp.mean(numerator * numerator, axis=-1, keepdims=True)
    hidden = (
        (numerator * lax.rsqrt(mean_square + 1e-05) * gain_mine)
        .astype(jnp.bfloat16)
        .reshape(tok_rows, value_cols)
    )
    out_mine = lax.dynamic_slice_in_dim(w_out, my_group * value_cols, value_cols, 0)
    partial_value = jnp.dot(hidden, out_mine, preferred_element_type=jnp.float32)
    partial_value = lax.optimization_barrier(partial_value.astype(jnp.bfloat16)).astype(jnp.float32)
    mixed = lax.psum_scatter(
        partial_value.astype(jnp.bfloat16), "chan", scatter_dimension=1, tiled=True
    )
    return mixed


def solution(mesh):
    return jax.shard_map(
        per_device,
        mesh=mesh,
        in_specs=(P("seq", "chan"), P(), P(), P(None, "chan"), P(), P()),
        out_specs=P("seq", "chan"),
        check_vma=False,
    )
```

profile of v0, /device:TPU:2, one launch (start us, length us, event | category | flops | bytes accessed | tf_op | source)
XLA Modules:
  0.0 357.5 jit_solution(1797674125439511556)
XLA Ops:
  6.5 0.0 copy-start
  6.5 0.0 all-gather.7.cloned.1.call-start
  6.5 0.7 all-gather.7.cloned.1.call-update
  7.3 0.0 all-gather.9.cloned.1.call-start
  7.3 0.8 dynamic_slice.14
  8.1 0.2 iota_compare_fusion
  8.3 96.7 %all-gather.7.cloned.1.call-done = bf16[3584,2048]{1,0:T(8,128)(2,1)} async-done(((bf16[3584,128]{1,0:T(8,128)(2,1)}), bf16[3584,2048]{1,0:T(8,128)(2,1)}) %all-gather.7.cloned.1.call-update) | async-done | bytes 14680080 | tf_op jit(solution)/shard_map/all_gather | solution.py:36
  105.0 9.2 %fusion.51 = (bf16[128]{0:T(256)(128)(2,1)S(1)}, bf16[3584,128]{1,0:T(8,128)(2,1)S(1)}) fusion(bf16[3584,2048]{1,0:T(8,128)(2,1)} %all-gather.7.cloned.1.call-done, bf16[2048,128]{1,0:T(8,128)(2,1)} %param.9), kind=kOutput, calls=%fused_computation.68 | convolution fusion | flops 1879965568 | bytes 16122112 | tf_op jit(solution)/shard_map/dot_general | solution.py:39
  114.3 0.1 convert_reduce_fusion
  114.4 0.0 copy-done
  114.4 9.4 %convolution_convert_fusion.2 = bf16[16,3584]{1,0:T(8,128)(2,1)S(1)} fusion(bf16[3584,2048]{1,0:T(8,128)(2,1)} %all-gather.7.cloned.1.call-done, bf16[2048,256]{1,0:T(8,128)(2,1)S(1)} %copy-done, s32[]{:T(128)S(6)} %select_n.25), kind=kOutput, calls=%fused_computation.3 | convolution fusion | flops 234938368 | bytes 15319044 | tf_op jit(solution)/shard_map/dot_general | solution.py:39
  123.8 0.5 fusion.50
  124.4 20.3 %all-gather.3 = bf16[16,1,128]{2,1,0:T(2,128)(2,1)S(1)} all-gather(bf16[1,1,128]{2,1,0:T(2,128)(2,1)S(1)} %bitcast.100), channel_id=2, replica_groups=mesh['seq'=16,'chan'=16] {'seq'}, dimensions={0}, use_global_device_ids=true | all-gather | bytes 4352 | tf_op jit(solution)/shard_map/all_gather | solution.py:59
  144.7 0.1 fusion.32
  144.8 0.0 copy-start.3
  144.8 21.4 %all-gather.1 = bf16[256,128]{1,0:T(8,128)(2,1)S(1)} all-gather(bf16[16,128]{1,0:T(8,128)(2,1)S(1)} %get-tuple-element.7), channel_id=3, replica_groups=mesh['seq'=16,'chan'=16] {'seq'}, dimensions={0}, use_global_device_ids=true | all-gather | bytes 69632 | tf_op jit(solution)/shard_map/all_gather | solution.py:62
  166.2 0.4 multiply_multiply_fusion.1
  166.6 2.5 fusion.49
  169.0 0.0 copy-done.3
  169.0 0.0 all-gather.9.cloned.1.call-update
  169.1 0.0 reduce-scatter.4.cloned.1.call-start
  169.1 0.4 fusion.8
  169.5 0.0 copy-start.2
  169.6 0.1 fusion.20
  169.7 0.1 fusion.37
  169.8 0.0 slice-start.1
  169.8 9.6 %convolution_convert_fusion.3 = bf16[16,3584]{1,0:T(8,128)(2,1)S(1)} fusion(bf16[3584,2048]{1,0:T(8,128)(2,1)} %all-gather.7.cloned.1.call-done, bf16[2048,256]{1,0:T(8,128)(2,1)} %param.7, s32[]{:T(128)S(6)} %select_n.25), kind=kOutput, calls=%fused_computation.4 | convolution fusion | flops 234938368 | bytes 15319044 | tf_op jit(solution)/shard_map/dot_general | solution.py:39
  179.4 0.0 copy-done.2
  179.4 0.0 slice-done.1
  179.4 0.0 slice-start
  179.4 2.9 fusion.16
  182.3 2.2 multiply_multiply_fusion
  184.5 29.4 %all-gather.9.cloned.1.call-done = bf16[4096,128]{1,0:T(8,128)(2,1)} async-done(((bf16[256,128]{1,0:T(8,128)(2,1)}), bf16[4096,128]{1,0:T(8,128)(2,1)}) %all-gather.9.cloned.1.call-update) | async-done | bytes 1048592 | tf_op jit(solution)/shard_map/all_gather | solution.py:65
  213.9 1.5 fusion
  215.4 0.0 slice-done
  215.4 5.6 %fusion.6 = f32[4,128,896]{2,1,0:T(8,128)} fusion(f32[4,896,256]{1,2,0:T(8,128)} %bitcast.84, f32[3,1,256,128]{3,2,0,1:T(8,128)S(1)} %slice-done, f32[256,128]{1,0:T(8,128)S(1)} %fusion), kind=kOutput, calls=%fused_computation.20 | convolution fusion | flops 1409417216 | bytes 6029312 | tf_op jit(solution)/shard_map/bthf,bhfe->bthe/dot_general | solution.py:93
  221.0 8.5 %multiply_reduce_fusion = (f32[4,896]{1,0:T(4,128)S(1)}, f32[4,896,1,128]{1,3,0,2:T(8,128)}) fusion(f32[4,128,896]{2,1,0:T(8,128)} %fusion.6, f32[4,128,896]{2,1,0:T(8,128)} %fusion.16, f32[4,128]{1,0:T(4,128)S(1)} %add_bitcast_fusion, bf16[4,896,128]{2,1,0:T(8,128)(2,1)S(1)} %bitcast.88, pred[896,896]{1,0:T(8,128)(4,1)S(1)} %iota_compare_fusion, ...), kind=kOutput, calls=%fused_computation.18 | convolution fusion | flops 949613056 | bytes 7471104 | tf_op jit(solution)/shard_map/bhts,bshe->bthe/dot_general | solution.py:100
  229.5 1.8 copy.41
  231.3 0.5 fusion.3
  231.9 8.3 %convolution_convert_fusion = bf16[3584,2048]{1,0:T(8,128)(2,1)} fusion(bf16[3584,128]{1,0:T(8,128)(2,1)S(1)} %fusion.3, bf16[2048,2048]{1,0:T(8,128)(2,1)} %param.10, s32[]{:T(128)S(6)} %select_n.30), kind=kOutput, calls=%fused_computation | convolution fusion | flops 1886388224 | bytes 16121860 | tf_op jit(solution)/shard_map/dot_general | solution.py:112
  240.2 18.8 %copy.45 = bf16[3584,2048]{0,1:T(8,128)(2,1)} copy(bf16[3584,2048]{1,0:T(8,128)(2,1)} %convolution_convert_fusion) | data formatting | bytes 29360128
  259.0 0.0 reduce-scatter.4.cloned.1.call-update
  259.0 0.0 copy-start.1
  259.0 89.8 %reduce-scatter.4.cloned.1.call-done = bf16[128,3584]{1,0:T(8,128)(2,1)} async-done(((bf16[2048,3584]{1,0:T(8,128)(2,1)}), bf16[128,3584]{1,0:T(8,128)(2,1)}) %reduce-scatter.4.cloned.1.call-update) | async-done | bytes 917520
  348.8 2.2 copy.46
  351.0 0.0 copy-done.1
  (7 shorter events, 0.1 us)
Async XLA Ops:
  6.5 107.9 %copy-start = (bf16[2048,256]{1,0:T(8,128)(2,1)S(1)}, bf16[2048,256]{1,0:T(8,128)(2,1)}, u32[]{:S(2)}) copy-start(bf16[2048,256]{1,0:T(8,128)(2,1)} %param.8) | copy-start | bytes 3145732
  6.5 98.5 %all-gather.7.cloned.1.call-start = ((), (), s32[]{:S(2)}) async-start(), calls=%async_computation.1 | async-start | bytes 15597568 | tf_op jit(solution)/shard_map/all_gather | solution.py:36
  7.3 206.7 %all-gather.9.cloned.1.call-start = ((), (), s32[]{:S(2)}) async-start(), calls=%async_computation.2 | async-start | bytes 1114112 | tf_op jit(solution)/shard_map/all_gather | solution.py:65
  144.8 24.3 %copy-start.3 = (f32[4,1,16,128]{3,2,0,1:T(8,128)}, f32[4,1,16,128]{3,2,0,1:T(8,128)S(1)}, u32[]{:S(2)}) copy-start(f32[4,1,16,128]{3,2,0,1:T(8,128)S(1)} %fusion.32) | copy-start | bytes 98308
  169.1 179.7 %reduce-scatter.4.cloned.1.call-start = ((), (), s32[]{:S(2)}) async-start(), calls=%async_computation.3 | async-start | bytes 15597568
  169.5 9.9 %copy-start.2 = (f32[4,1,256,128]{3,2,0,1:T(8,128)}, f32[4,1,256,128]{3,2,0,1:T(8,128)S(1)}, u32[]{:S(2)}) copy-start(f32[4,1,256,128]{3,2,0,1:T(8,128)S(1)} %fusion.8) | copy-start | bytes 1572868
  169.8 9.6 %slice-start.1 = ((f32[4,1,16,128]{3,2,0,1:T(8,128)}), f32[3,1,16,128]{3,2,0,1:T(8,128)S(1)}, s32[]{:S(2)}) async-start(f32[4,1,16,128]{3,2,0,1:T(8,128)} %copy-done.3), calls=%async_computation.5 | async-start | bytes 49152 | tf_op jit(solution)/shard_map/slice | solution.py:84
  179.4 36.0 %slice-start = ((f32[4,1,256,128]{3,2,0,1:T(8,128)}), f32[3,1,256,128]{3,2,0,1:T(8,128)S(1)}, s32[]{:S(2)}) async-start(f32[4,1,256,128]{3,2,0,1:T(8,128)} %copy-done.2), calls=%async_computation.4 | async-start | bytes 786432 | tf_op jit(solution)/shard_map/slice | solution.py:84
  259.0 92.0 %copy-start.1 = (bf16[2048,256]{1,0:T(8,128)(2,1)S(1)}, bf16[2048,256]{1,0:T(8,128)(2,1)}, u32[]{:S(2)}) copy-start(bf16[2048,256]{1,0:T(8,128)(2,1)} %param.8) | copy-start | bytes 3145732
Sparse Core Ops, SparseCore 0:
  9.1 95.8 all-gather.6
  169.2 44.6 all-gather.8
  259.1 89.6 reduce-scatter.3
where the time goes:
time: 358 us
  waiting for transfers between devices  217 us (61%)
  matrix products  56.4 us (16%)
  blocking collectives  41.7 us (12%)
  local copies, waits for them, and re-layouts  23.6 us (7%)
  between operations  13.3 us (4%)
  other arithmetic  5.75 us (2%)
    all_gather x1, waiting for transfers between devices, per_device(): piece = lax.all_gather(tokens, 'chan', axis=1, tiled=True)  96.7 us
    unnamed x4, waiting for transfers between devices  90.5 us
    all_gather x1, waiting for transfers between devices, per_device(): lax.all_gather(slab_total[2][None].astype(jnp.bfloat16), 'seq', axis=0, t...  29.4 us
    dot_general x3, matrix products, per_device(): jnp.dot(piece, weight, preferred_element_type=jnp.float32)  28.2 us
    all_gather x1, blocking collectives, per_device(): lax.all_gather(slab_total[1][None].astype(jnp.bfloat16), 'seq', axis=0, t...  21.4 us
    unnamed x10, local copies, waits for them, and re-layouts  21 us
    all_gather x1, blocking collectives, per_device(): lax.all_gather(slab_total[0][None].astype(jnp.bfloat16), 'seq', axis=0, t...  20.3 us
    dot_general x1, matrix products, per_device(): jnp.einsum('bhts,bshe->bthe', weights, value_blocks, preferred_element_ty...  8.45 us
  transfers between devices with their start and end apart: 3, of which 3 were waited for; matrix products, arithmetic and copies ran while one was open for 5% of the time, Pallas kernels for 0%

commit v1 on v0

--- a/solution.py
+++ b/solution.py
@@ -33,7 +33,16 @@
         jnp.zeros((tok_rows, query_cols), jnp.float32),
         jnp.zeros((tok_rows, value_cols), jnp.float32),
     )
-    piece = lax.all_gather(tokens, "chan", axis=1, tiled=True)
+    full_n = lax.psum(1, "chan")
+    windows = [(ix, (ix + 1) % full_n) for ix in range(full_n)]
+    rack = [(ix, (ix - 1) % full_n) for ix in range(full_n)]
+    block_now, s_next = ([tokens], [tokens])
+    for _ in range(full_n // 2):
+        block_now.append(lax.ppermute(block_now[-1], "chan", windows))
+    for _ in range((full_n - 1) // 2):
+        s_next.append(lax.ppermute(s_next[-1], axis_name="chan", perm=rack))
+    g_now = jnp.concatenate([*block_now[::-1], *s_next[1:]], axis=1)
+    piece = jnp.roll(g_now, (lax.axis_index("chan") - full_n // 2) * tokens.shape[1], axis=1)
     query_sum, key_sum, value_sum = tuple(
         (
             jnp.dot(piece, weight, preferred_element_type=jnp.float32)

time: 358 us -> 402 us (1.12)
  local copies, waits for them, and re-layouts: 23.6 us -> 83.1 us
  waiting for transfers between devices: 217 us -> 179 us
  starting transfers between devices: 0.08 us -> 21.6 us
    all_gather x1 -> x0, waiting for transfers between devices: 96.7 us -> none  [per_device(): piece = lax.all_gather(tokens, 'chan', axis=1, tiled=True)]
    ppermute x0 -> x15, waiting for transfers between devices: none -> 89.9 us  [the longest x8 85.5 us: per_device(): block_now.append(lax.ppermute(block_now[-1], 'chan', windows))]
    unnamed x10 -> x69, local copies, waits for them, and re-layouts: 21 us -> 79.2 us
    all_gather x1, waiting for transfers between devices: 29.4 us -> 0.01 us  [per_device(): lax.all_gather(slab_total[2][None].astype(jnp.bfloat16), 'seq', axis=0, t...]
    ppermute x0 -> x15, starting transfers between devices: none -> 21.5 us  [the longest x7 21.5 us: per_device(): s_next.append(lax.ppermute(s_next[-1], axis_name='chan', perm=rack))]
    unnamed x4 -> x3, waiting for transfers between devices: 90.5 us -> 89 us
  transfers between devices with their start and end apart: 3 -> 17, of which waited for: 3 -> 14; matrix products, arithmetic and copies ran while one was open for 5% -> 12% of each run, Pallas kernels for 0% -> 0%
where the time goes in v1:
time: 402 us; the launch traced here: 400 us
  waiting for transfers between devices  179 us (45%)
  local copies, waits for them, and re-layouts  83.1 us (21%)
  matrix products  54.2 us (13%)
  blocking collectives  42.2 us (10%)
  starting transfers between devices  21.6 us (5%)
  between operations  13.6 us (3%)
  other arithmetic  6.48 us (2%)
    unnamed x3, waiting for transfers between devices  89 us
    ppermute x8, waiting for transfers between devices, per_device(): block_now.append(lax.ppermute(block_now[-1], 'chan', windows))  85.5 us
    unnamed x69, local copies, waits for them, and re-layouts  79.2 us
    dot_general x3, matrix products, per_device(): jnp.dot(piece, weight, preferred_element_type=jnp.float32)  26.2 us
    all_gather x1, blocking collectives, per_device(): lax.all_gather(slab_total[1][None].astype(jnp.bfloat16), 'seq', axis=0, t...  21.6 us
    ppermute x7, starting transfers between devices, per_device(): s_next.append(lax.ppermute(s_next[-1], axis_name='chan', perm=rack))  21.5 us
    all_gather x1, blocking collectives, per_device(): lax.all_gather(slab_total[0][None].astype(jnp.bfloat16), 'seq', axis=0, t...  20.6 us
    dot_general x1, matrix products, per_device(): jnp.dot(hidden, out_mine, preferred_element_type=jnp.float32)  8.29 us
  transfers between devices with their start and end apart: 17, of which 14 were waited for; matrix products, arithmetic and copies ran while one was open for 12% of the time, Pallas kernels for 0%

profile of v1, /device:TPU:2, one launch (start us, length us, event | category | flops | bytes accessed | tf_op | source)
XLA Modules:
  0.0 400.0 jit_solution(15196121008816614359)
XLA Ops:
  6.6 16.6 %collective-permute-done = bf16[3584,128]{1,0:T(8,128)(2,1)S(1)} collective-permute-done((bf16[3584,128]{1,0:T(8,128)(2,1)}, bf16[3584,128]{1,0:T(8,128)(2,1)S(1)}, u32[]{:S(2)}, u32[]{:S(2)}) %collective-permute-start) | collective-permute-done | bytes 917536 | tf_op jit(solution)/shard_map/ppermute | solution.py:41
  23.2 3.0 collective-permute-start.8
  26.1 11.2 %collective-permute-done.1 = bf16[3584,128]{1,0:T(8,128)(2,1)} collective-permute-done((bf16[3584,128]{1,0:T(8,128)(2,1)S(1)}, bf16[3584,128]{1,0:T(8,128)(2,1)}, u32[]{:S(2)}, u32[]{:S(2)}) %collective-permute-start.1) | collective-permute-done | bytes 917536 | tf_op jit(solution)/shard_map/ppermute | solution.py:41
  37.3 3.1 collective-permute-start.9
  40.5 11.1 %collective-permute-done.2 = bf16[3584,128]{1,0:T(8,128)(2,1)S(1)} collective-permute-done((bf16[3584,128]{1,0:T(8,128)(2,1)}, bf16[3584,128]{1,0:T(8,128)(2,1)S(1)}, u32[]{:S(2)}, u32[]{:S(2)}) %collective-permute-start.2) | collective-permute-done | bytes 917536 | tf_op jit(solution)/shard_map/ppermute | solution.py:41
  52.8 2.9 collective-permute-start.10
  55.7 9.9 %collective-permute-done.3 = bf16[3584,128]{1,0:T(8,128)(2,1)S(1)} collective-permute-done((bf16[3584,128]{1,0:T(8,128)(2,1)S(1)}, bf16[3584,128]{1,0:T(8,128)(2,1)S(1)}, u32[]{:S(2)}, u32[]{:S(2)}) %collective-permute-start.3) | collective-permute-done | bytes 917536 | tf_op jit(solution)/shard_map/ppermute | solution.py:41
  66.6 3.1 collective-permute-start.11
  69.7 9.9 %collective-permute-done.4 = bf16[3584,128]{1,0:T(8,128)(2,1)S(1)} collective-permute-done((bf16[3584,128]{1,0:T(8,128)(2,1)S(1)}, bf16[3584,128]{1,0:T(8,128)(2,1)S(1)}, u32[]{:S(2)}, u32[]{:S(2)}) %collective-permute-start.4) | collective-permute-done | bytes 917536 | tf_op jit(solution)/shard_map/ppermute | solution.py:41
  81.5 3.1 collective-permute-start.12
  84.7 9.0 %collective-permute-done.5 = bf16[3584,128]{1,0:T(8,128)(2,1)S(1)} collective-permute-done((bf16[3584,128]{1,0:T(8,128)(2,1)S(1)}, bf16[3584,128]{1,0:T(8,128)(2,1)S(1)}, u32[]{:S(2)}, u32[]{:S(2)}) %collective-permute-start.5) | collective-permute-done | bytes 917536 | tf_op jit(solution)/shard_map/ppermute | solution.py:41
  95.6 3.2 collective-permute-start.13
  98.8 9.0 %collective-permute-done.6 = bf16[3584,128]{1,0:T(8,128)(2,1)} collective-permute-done((bf16[3584,128]{1,0:T(8,128)(2,1)S(1)}, bf16[3584,128]{1,0:T(8,128)(2,1)}, u32[]{:S(2)}, u32[]{:S(2)}) %collective-permute-start.6) | collective-permute-done | bytes 917536 | tf_op jit(solution)/shard_map/ppermute | solution.py:41
  110.0 3.1 collective-permute-start.14
  113.1 9.0 %collective-permute-done.7 = bf16[3584,128]{1,0:T(8,128)(2,1)} collective-permute-done((bf16[3584,128]{1,0:T(8,128)(2,1)}, bf16[3584,128]{1,0:T(8,128)(2,1)}, u32[]{:S(2)}, u32[]{:S(2)}) %collective-permute-start.7) | collective-permute-done | bytes 917536 | tf_op jit(solution)/shard_map/ppermute | solution.py:41
  122.1 2.2 constant_dynamic-update-slice_fusion.31
  124.4 2.2 constant_dynamic-update-slice_fusion.30
  126.6 2.2 constant_dynamic-update-slice_fusion.29
  128.8 2.2 constant_dynamic-update-slice_fusion.28
  131.0 2.2 constant_dynamic-update-slice_fusion.27
  133.2 2.2 constant_dynamic-update-slice_fusion.26
  135.5 2.3 constant_dynamic-update-slice_fusion.25
  138.7 2.2 constant_dynamic-update-slice_fusion.23
  140.9 2.2 constant_dynamic-update-slice_fusion.22
  143.1 2.2 constant_dynamic-update-slice_fusion.21
  145.3 2.2 constant_dynamic-update-slice_fusion.20
  147.5 2.3 constant_dynamic-update-slice_fusion.19
  149.8 2.2 constant_dynamic-update-slice_fusion.18
  152.0 2.2 constant_dynamic-update-slice_fusion.17
  155.3 2.2 constant_dynamic-update-slice_fusion.15
  157.5 2.2 constant_dynamic-update-slice_fusion.14
  164.0 2.2 constant_dynamic-update-slice_fusion.9
  168.4 2.2 constant_dynamic-update-slice_fusion.6
  173.8 2.2 constant_dynamic-update-slice_fusion.2
  176.1 2.3 constant_dynamic-update-slice_fusion.1
  179.4 7.8 %fusion.67 = (bf16[128]{0:T(256)(128)(2,1)S(1)}, bf16[3584,128]{1,0:T(8,128)(2,1)S(1)}) fusion(bf16[2048,128]{1,0:T(8,128)(2,1)S(1)} %copy-done.17, bf16[3584,4096]{1,0:T(8,128)(2,1)} %constant_dynamic-update-slice_fusion, s32[]{:T(128)S(6)} %select_n.39), kind=kOutput, calls=%fused_computation.107 | convolution fusion | flops 1879965568 | bytes 16122116 | tf_op jit(solution)/shard_map/dot_general | solution.py:48
  187.2 9.2 %fusion.12 = bf16[3584,16]{0,1:T(8,128)(2,1)S(1)} fusion(bf16[3584,4096]{1,0:T(8,128)(2,1)} %constant_dynamic-update-slice_fusion, s32[]{:T(128)S(6)} %select_n.39, bf16[2048,256]{1,0:T(8,128)(2,1)S(1)} %copy-done, s32[]{:T(128)S(6)} %select_n.40), kind=kOutput, calls=%fused_computation.10 | convolution fusion | flops 234938368 | bytes 15319048 | tf_op jit(solution)/shard_map/dot_general | solution.py:48
  197.5 2.5 fusion.65
  200.5 20.6 %all-gather.3 = bf16[16,1,128]{2,1,0:T(2,128)(2,1)S(1)} all-gather(bf16[1,1,128]{2,1,0:T(2,128)(2,1)S(1)} %bitcast.95), channel_id=2, replica_groups=mesh['seq'=16,'chan'=16] {'seq'}, dimensions={0}, use_global_device_ids=true | all-gather | bytes 4352 | tf_op jit(solution)/shard_map/all_gather | solution.py:68
  221.1 21.6 %all-gather.1 = bf16[256,128]{1,0:T(8,128)(2,1)S(1)} all-gather(bf16[16,128]{1,0:T(8,128)(2,1)S(1)} %get-tuple-element.7), channel_id=3, replica_groups=mesh['seq'=16,'chan'=16] {'seq'}, dimensions={0}, use_global_device_ids=true | all-gather | bytes 69632 | tf_op jit(solution)/shard_map/all_gather | solution.py:71
  242.9 9.3 %fusion.9 = bf16[3584,16]{0,1:T(8,128)(2,1)S(1)} fusion(bf16[3584,4096]{1,0:T(8,128)(2,1)} %constant_dynamic-update-slice_fusion, s32[]{:T(128)S(6)} %select_n.39, bf16[2048,256]{1,0:T(8,128)(2,1)} %param.7, s32[]{:T(128)S(6)} %select_n.40), kind=kOutput, calls=%fused_computation.9 | convolution fusion | flops 234938368 | bytes 15319048 | tf_op jit(solution)/shard_map/dot_general | solution.py:48
  252.2 2.9 fusion.31
  258.8 5.6 %fusion.21 = f32[4,128,896]{2,1,0:T(8,128)} fusion(f32[4,896,256]{1,2,0:T(8,128)} %bitcast.79, f32[3,1,256,128]{3,2,0,1:T(8,128)S(1)} %slice.13, f32[256,128]{1,0:T(8,128)S(1)} %fusion.15), kind=kOutput, calls=%fused_computation.26 | convolution fusion | flops 1409417216 | bytes 6029312 | tf_op jit(solution)/shard_map/bthf,bhfe->bthe/dot_general | solution.py:102
  264.4 8.2 %multiply_reduce_fusion = (f32[4,896]{1,0:T(4,128)S(1)}, f32[4,896,1,128]{1,3,0,2:T(8,128)}) fusion(f32[4,128,896]{2,1,0:T(8,128)} %fusion.21, f32[4,128,896]{2,1,0:T(8,128)} %fusion.31, f32[4,128]{1,0:T(4,128)S(1)} %add_bitcast_fusion, bf16[4,896,128]{2,1,0:T(8,128)(2,1)S(1)} %bitcast.83, pred[896,896]{1,0:T(8,128)(4,1)S(1)} %copy-done.16, ...), kind=kOutput, calls=%fused_computation.24 | convolution fusion | flops 949613056 | bytes 7471104 | tf_op jit(solution)/shard_map/bhts,bshe->bthe/dot_general | solution.py:109
  274.9 8.3 %convolution_convert_fusion = bf16[3584,2048]{1,0:T(8,128)(2,1)} fusion(bf16[3584,128]{1,0:T(8,128)(2,1)S(1)} %fusion.18, bf16[2048,2048]{1,0:T(8,128)(2,1)} %param.10, s32[]{:T(128)S(6)} %select_n.45), kind=kOutput, calls=%fused_computation | convolution fusion | flops 1886388224 | bytes 16121860 | tf_op jit(solution)/shard_map/dot_general | solution.py:121
  283.2 18.7 %copy.45 = bf16[3584,2048]{0,1:T(8,128)(2,1)} copy(bf16[3584,2048]{1,0:T(8,128)(2,1)} %convolution_convert_fusion) | data formatting | bytes 29360128
  302.0 89.0 %reduce-scatter.4.cloned.1.call-done = bf16[128,3584]{1,0:T(8,128)(2,1)} async-done(((bf16[2048,3584]{1,0:T(8,128)(2,1)}), bf16[128,3584]{1,0:T(8,128)(2,1)}) %reduce-scatter.4.cloned.1.call-update) | async-done | bytes 917520
  391.0 2.2 copy.46
  (90 shorter events, 29.1 us)
Async XLA Ops:
  6.5 180.7 %copy-start = (bf16[2048,256]{1,0:T(8,128)(2,1)S(1)}, bf16[2048,256]{1,0:T(8,128)(2,1)}, u32[]{:S(2)}) copy-start(bf16[2048,256]{1,0:T(8,128)(2,1)} %param.8) | copy-start | bytes 3145732
  6.5 160.7 %copy-start.1 = (bf16[3584,128]{1,0:T(8,128)(2,1)S(1)}, bf16[3584,128]{1,0:T(8,128)(2,1)}, u32[]{:S(2)}) copy-start(bf16[3584,128]{1,0:T(8,128)(2,1)} %param.6) | copy-start | bytes 2752516
  6.5 250.7 %all-gather.6.cloned.1.call-start = ((), (), s32[]{:S(2)}) async-start(), calls=%async_computation.1 | async-start | bytes 1114112 | tf_op jit(solution)/shard_map/all_gather | solution.py:74
  6.5 16.6 %collective-permute-start = (bf16[3584,128]{1,0:T(8,128)(2,1)}, bf16[3584,128]{1,0:T(8,128)(2,1)S(1)}, u32[]{:S(2)}, u32[]{:S(2)}) collective-permute-start(bf16[3584,128]{1,0:T(8,128)(2,1)} %param.6), channel_id=1, source_target_pairs={{0,1},{1,2},{2,3},{3,4},{4,5},{5,6},{6,7},{7,8},{8,9},{9,10},{10,1... | collective-permute-start | bytes 2752520 | tf_op jit(solution)/shard_map/ppermute | solution.py:41
  23.2 14.1 %collective-permute-start.1 = (bf16[3584,128]{1,0:T(8,128)(2,1)S(1)}, bf16[3584,128]{1,0:T(8,128)(2,1)}, u32[]{:S(2)}, u32[]{:S(2)}) collective-permute-start(bf16[3584,128]{1,0:T(8,128)(2,1)S(1)} %collective-permute-done), channel_id=1, source_target_pairs={{0,1},{1,2},{2,3},{3,4},{4,5},{5,6},{6,7},{7,8},{8,9},{9,10},{10,1... | collective-permute-start | bytes 2752520 | tf_op jit(solution)/shard_map/ppermute | solution.py:41
  23.2 14.2 %collective-permute-start.8 = (bf16[3584,128]{1,0:T(8,128)(2,1)}, bf16[3584,128]{1,0:T(8,128)(2,1)}, u32[]{:S(2)}, u32[]{:S(2)}) collective-permute-start(bf16[3584,128]{1,0:T(8,128)(2,1)} %param.6), channel_id=1, source_target_pairs={{0,15},{1,0},{2,1},{3,2},{4,3},{5,4},{6,5},{7,6},{8,7},{9,8},{10,9... | collective-permute-start | bytes 2752520 | tf_op jit(solution)/shard_map/ppermute | solution.py:43
  37.3 14.2 %collective-permute-start.2 = (bf16[3584,128]{1,0:T(8,128)(2,1)}, bf16[3584,128]{1,0:T(8,128)(2,1)S(1)}, u32[]{:S(2)}, u32[]{:S(2)}) collective-permute-start(bf16[3584,128]{1,0:T(8,128)(2,1)} %collective-permute-done.1), channel_id=1, source_target_pairs={{0,1},{1,2},{2,3},{3,4},{4,5},{5,6},{6,7},{7,8},{8,9},{9,10},{10,1... | collective-permute-start | bytes 2752520 | tf_op jit(solution)/shard_map/ppermute | solution.py:41
  37.3 14.3 %collective-permute-start.9 = (bf16[3584,128]{1,0:T(8,128)(2,1)}, bf16[3584,128]{1,0:T(8,128)(2,1)S(1)}, u32[]{:S(2)}, u32[]{:S(2)}) collective-permute-start(bf16[3584,128]{1,0:T(8,128)(2,1)} %collective-permute-done.8), channel_id=1, source_target_pairs={{0,15},{1,0},{2,1},{3,2},{4,3},{5,4},{6,5},{7,6},{8,7},{9,8},{10,9... | collective-permute-start | bytes 2752520 | tf_op jit(solution)/shard_map/ppermute | solution.py:43
  51.5 15.1 %copy-start.4 = (bf16[3584,128]{1,0:T(8,128)(2,1)}, bf16[3584,128]{1,0:T(8,128)(2,1)S(1)}, u32[]{:S(2)}) copy-start(bf16[3584,128]{1,0:T(8,128)(2,1)S(1)} %collective-permute-done.2) | copy-start | bytes 2752516
  51.5 14.0 %collective-permute-start.3 = (bf16[3584,128]{1,0:T(8,128)(2,1)S(1)}, bf16[3584,128]{1,0:T(8,128)(2,1)S(1)}, u32[]{:S(2)}, u32[]{:S(2)}) collective-permute-start(bf16[3584,128]{1,0:T(8,128)(2,1)S(1)} %collective-permute-done.2), channel_id=1, source_target_pairs={{0,1},{1,2},{2,3},{3,4},{4,5},{5,6},{6,7},{7,8},{8,9},{9,10},{10,1... | collective-permute-start | bytes 2752520 | tf_op jit(solution)/shard_map/ppermute | solution.py:41
  51.7 1.1 copy-start.2
  52.8 13.8 %collective-permute-start.10 = (bf16[3584,128]{1,0:T(8,128)(2,1)S(1)}, bf16[3584,128]{1,0:T(8,128)(2,1)S(1)}, u32[]{:S(2)}, u32[]{:S(2)}) collective-permute-start(bf16[3584,128]{1,0:T(8,128)(2,1)S(1)} %collective-permute-done.9), channel_id=1, source_target_pairs={{0,15},{1,0},{2,1},{3,2},{4,3},{5,4},{6,5},{7,6},{8,7},{9,8},{10,9... | collective-permute-start | bytes 2752520 | tf_op jit(solution)/shard_map/ppermute | solution.py:43
  65.6 30.0 %copy-start.10 = (bf16[3584,128]{1,0:T(8,128)(2,1)}, bf16[3584,128]{1,0:T(8,128)(2,1)S(1)}, u32[]{:S(2)}) copy-start(bf16[3584,128]{1,0:T(8,128)(2,1)S(1)} %collective-permute-done.3) | copy-start | bytes 2752516
  65.6 14.0 %collective-permute-start.4 = (bf16[3584,128]{1,0:T(8,128)(2,1)S(1)}, bf16[3584,128]{1,0:T(8,128)(2,1)S(1)}, u32[]{:S(2)}, u32[]{:S(2)}) collective-permute-start(bf16[3584,128]{1,0:T(8,128)(2,1)S(1)} %collective-permute-done.3), channel_id=1, source_target_pairs={{0,1},{1,2},{2,3},{3,4},{4,5},{5,6},{6,7},{7,8},{8,9},{9,10},{10,1... | collective-permute-start | bytes 2752520 | tf_op jit(solution)/shard_map/ppermute | solution.py:41
  66.6 3.1 copy-start.6
  66.6 14.0 %collective-permute-start.11 = (bf16[3584,128]{1,0:T(8,128)(2,1)S(1)}, bf16[3584,128]{1,0:T(8,128)(2,1)S(1)}, u32[]{:S(2)}, u32[]{:S(2)}) collective-permute-start(bf16[3584,128]{1,0:T(8,128)(2,1)S(1)} %collective-permute-done.10), channel_id=1, source_target_pairs={{0,15},{1,0},{2,1},{3,2},{4,3},{5,4},{6,5},{7,6},{8,7},{9,8},{10,9... | collective-permute-start | bytes 2752520 | tf_op jit(solution)/shard_map/ppermute | solution.py:43
  79.6 19.2 %copy-start.12 = (bf16[3584,128]{1,0:T(8,128)(2,1)}, bf16[3584,128]{1,0:T(8,128)(2,1)S(1)}, u32[]{:S(2)}) copy-start(bf16[3584,128]{1,0:T(8,128)(2,1)S(1)} %collective-permute-done.4) | copy-start | bytes 2752516
  79.6 14.0 %collective-permute-start.5 = (bf16[3584,128]{1,0:T(8,128)(2,1)S(1)}, bf16[3584,128]{1,0:T(8,128)(2,1)S(1)}, u32[]{:S(2)}, u32[]{:S(2)}) collective-permute-start(bf16[3584,128]{1,0:T(8,128)(2,1)S(1)} %collective-permute-done.4), channel_id=1, source_target_pairs={{0,1},{1,2},{2,3},{3,4},{4,5},{5,6},{6,7},{7,8},{8,9},{9,10},{10,1... | collective-permute-start | bytes 2752520 | tf_op jit(solution)/shard_map/ppermute | solution.py:41
  80.6 0.9 copy-start.8
  81.5 14.0 %collective-permute-start.12 = (bf16[3584,128]{1,0:T(8,128)(2,1)S(1)}, bf16[3584,128]{1,0:T(8,128)(2,1)}, u32[]{:S(2)}, u32[]{:S(2)}) collective-permute-start(bf16[3584,128]{1,0:T(8,128)(2,1)S(1)} %collective-permute-done.11), channel_id=1, source_target_pairs={{0,15},{1,0},{2,1},{3,2},{4,3},{5,4},{6,5},{7,6},{8,7},{9,8},{10,9... | collective-permute-start | bytes 2752520 | tf_op jit(solution)/shard_map/ppermute | solution.py:43
  93.6 14.1 %copy-start.14 = (bf16[3584,128]{1,0:T(8,128)(2,1)}, bf16[3584,128]{1,0:T(8,128)(2,1)S(1)}, u32[]{:S(2)}) copy-start(bf16[3584,128]{1,0:T(8,128)(2,1)S(1)} %collective-permute-done.5) | copy-start | bytes 2752516
  93.6 14.1 %collective-permute-start.6 = (bf16[3584,128]{1,0:T(8,128)(2,1)S(1)}, bf16[3584,128]{1,0:T(8,128)(2,1)}, u32[]{:S(2)}, u32[]{:S(2)}) collective-permute-start(bf16[3584,128]{1,0:T(8,128)(2,1)S(1)} %collective-permute-done.5), channel_id=1, source_target_pairs={{0,1},{1,2},{2,3},{3,4},{4,5},{5,6},{6,7},{7,8},{8,9},{9,10},{10,1... | collective-permute-start | bytes 2752520 | tf_op jit(solution)/shard_map/ppermute | solution.py:41
  95.6 14.5 %collective-permute-start.13 = (bf16[3584,128]{1,0:T(8,128)(2,1)}, bf16[3584,128]{1,0:T(8,128)(2,1)}, u32[]{:S(2)}, u32[]{:S(2)}) collective-permute-start(bf16[3584,128]{1,0:T(8,128)(2,1)} %collective-permute-done.12), channel_id=1, source_target_pairs={{0,15},{1,0},{2,1},{3,2},{4,3},{5,4},{6,5},{7,6},{8,7},{9,8},{10,9... | collective-permute-start | bytes 2752520 | tf_op jit(solution)/shard_map/ppermute | solution.py:43
  107.8 14.3 %collective-permute-start.7 = (bf16[3584,128]{1,0:T(8,128)(2,1)}, bf16[3584,128]{1,0:T(8,128)(2,1)}, u32[]{:S(2)}, u32[]{:S(2)}) collective-permute-start(bf16[3584,128]{1,0:T(8,128)(2,1)} %collective-permute-done.6), channel_id=1, source_target_pairs={{0,1},{1,2},{2,3},{3,4},{4,5},{5,6},{6,7},{7,8},{8,9},{9,10},{10,1... | collective-permute-start | bytes 2752520 | tf_op jit(solution)/shard_map/ppermute | solution.py:41
  107.8 51.9 %copy-start.15 = (bf16[3584,128]{1,0:T(8,128)(2,1)S(1)}, bf16[3584,128]{1,0:T(8,128)(2,1)}, u32[]{:S(2)}) copy-start(bf16[3584,128]{1,0:T(8,128)(2,1)} %copy-done.14) | copy-start | bytes 2752516
  107.8 53.1 %copy-start.13 = (bf16[3584,128]{1,0:T(8,128)(2,1)S(1)}, bf16[3584,128]{1,0:T(8,128)(2,1)}, u32[]{:S(2)}) copy-start(bf16[3584,128]{1,0:T(8,128)(2,1)} %copy-done.12) | copy-start | bytes 2752516
  107.8 54.1 %copy-start.11 = (bf16[3584,128]{1,0:T(8,128)(2,1)S(1)}, bf16[3584,128]{1,0:T(8,128)(2,1)}, u32[]{:S(2)}) copy-start(bf16[3584,128]{1,0:T(8,128)(2,1)} %copy-done.10) | copy-start | bytes 2752516
  107.8 55.1 %copy-start.5 = (bf16[3584,128]{1,0:T(8,128)(2,1)S(1)}, bf16[3584,128]{1,0:T(8,128)(2,1)}, u32[]{:S(2)}) copy-start(bf16[3584,128]{1,0:T(8,128)(2,1)} %copy-done.4) | copy-start | bytes 2752516
  107.8 62.8 %copy-start.3 = (bf16[3584,128]{1,0:T(8,128)(2,1)S(1)}, bf16[3584,128]{1,0:T(8,128)(2,1)}, u32[]{:S(2)}) copy-start(bf16[3584,128]{1,0:T(8,128)(2,1)} %copy-done.2) | copy-start | bytes 2752516
  107.8 63.9 %copy-start.7 = (bf16[3584,128]{1,0:T(8,128)(2,1)S(1)}, bf16[3584,128]{1,0:T(8,128)(2,1)}, u32[]{:S(2)}) copy-start(bf16[3584,128]{1,0:T(8,128)(2,1)} %copy-done.6) | copy-start | bytes 2752516
  107.8 65.0 %copy-start.9 = (bf16[3584,128]{1,0:T(8,128)(2,1)S(1)}, bf16[3584,128]{1,0:T(8,128)(2,1)}, u32[]{:S(2)}) copy-start(bf16[3584,128]{1,0:T(8,128)(2,1)} %copy-done.8) | copy-start | bytes 2752516
  109.9 69.6 %copy-start.17 = (bf16[2048,128]{1,0:T(8,128)(2,1)S(1)}, bf16[2048,128]{1,0:T(8,128)(2,1)}, u32[]{:S(2)}) copy-start(bf16[2048,128]{1,0:T(8,128)(2,1)} %param.9) | copy-start | bytes 1572868
  110.0 44.2 %collective-permute-start.14 = (bf16[3584,128]{1,0:T(8,128)(2,1)}, bf16[3584,128]{1,0:T(8,128)(2,1)S(1)}, u32[]{:S(2)}, u32[]{:S(2)}) collective-permute-start(bf16[3584,128]{1,0:T(8,128)(2,1)} %collective-permute-done.13), channel_id=1, source_target_pairs={{0,15},{1,0},{2,1},{3,2},{4,3},{5,4},{6,5},{7,6},{8,7},{9,8},{10,9... | collective-permute-start | bytes 2752520 | tf_op jit(solution)/shard_map/ppermute | solution.py:43
  187.2 77.1 %copy-start.16 = (pred[896,896]{1,0:T(8,128)(4,1)S(1)}, pred[896,896]{1,0:T(8,128)(4,1)}, u32[]{:S(2)}) copy-start(pred[896,896]{1,0:T(8,128)(4,1)} %iota_compare_fusion) | copy-start | bytes 2408452
  200.0 191.0 %reduce-scatter.4.cloned.1.call-start = ((), (), s32[]{:S(2)}) async-start(), calls=%async_computation.2 | async-start | bytes 15597568
Sparse Core Ops, SparseCore 0:
  200.1 47.8 all-gather.5
  302.1 88.8 reduce-scatter.3
